TPU v7x, 512 devices: a whole 4x4x16 slice. The times are simulated.
512 devices in a mesh: row: 64 (over z, y), col: 8 (over x, core).
Axes of the slice: x: 4, y: 4, z: 16, core: 2. Of those that a mesh axis runs over, the one named last changes fastest.
Arguments:
- amplitudes: bfloat16 [2048, 16384], P('row', 'col'), may hold values from -6 to 6
- integrals: bfloat16 [2048, 16384], P('col', 'row'), may hold values from -0.125 to 0.125
- amp_mask: int32 [64, 128], replicated, may hold values 0 or 1
- int_mask: int32 [64, 128], replicated, may hold values 0 or 1
Outputs:
- scaled_residual: float32 [16384, 16384], P('col', 'row')
- row_norm: float32 [16384], P('col')
Inputs may be any that keep to these rules, and one draw needn't show every extreme that they name: `amp_mask`: an entry of 1 keeps its tile, 0 drops it. `int_mask`: an entry of 1 keeps its tile, 0 drops it.
All inputs are finite; a program needn't handle non-finite values.
Results may differ from a plain program's by a relative error of at most 0.0003.
Values may be sent and summed in bfloat16 or wider, within the bound.
A program may use at most 64 MiB of HBM per device.

v0:
```python
import jax
import jax.numpy as jnp
from jax import lax
from jax.sharding import PartitionSpec as P

OCC = 128
TILE = 128


def contract(left, right):
    return lax.dot_general(
        left, right, (((0,), (0,)), ((), ())), preferred_element_type=jnp.float32
    )


def row_keep(table, start, count, block):
    blocks = table.shape[0]
    owners = (start + jnp.arange(count, dtype=jnp.int32)) // block
    onehot = (owners[:, None] == jnp.arange(blocks, dtype=jnp.int32)[None, :]).astype(jnp.bfloat16)
    picked = jnp.dot(onehot, table.astype(jnp.bfloat16), preferred_element_type=jnp.float32)
    return jnp.repeat(picked, TILE, axis=1).astype(jnp.bfloat16)


def local(amplitudes, integrals, amp_mask, int_mask):
    block, m_dev = amplitudes.shape
    ab_dev = integrals.shape[1]
    row_place = lax.axis_index("row")
    col_place = lax.axis_index("col")
    m_tiles = m_dev // TILE
    n_tiles = ab_dev // TILE
    occ_dev = m_dev // OCC
    amp_keep = lax.dynamic_slice_in_dim(amp_mask, col_place * m_tiles, m_tiles, 1)
    int_keep = lax.dynamic_slice_in_dim(int_mask, row_place * n_tiles, n_tiles, 1)
    own_amp = amplitudes * row_keep(amp_keep, row_place * block, block, block)
    stacked = own_amp[None]
    whole_int = lax.all_gather(integrals, "col", axis=0, tiled=True)
    whole_int = whole_int * row_keep(int_keep, 0, whole_int.shape[0], block)
    total = contract(lax.all_gather(stacked, "row", axis=1, tiled=True)[0], whole_int)
    cube = total.reshape(occ_dev, OCC, ab_dev)
    moved = lax.all_to_all(cube, "col", split_axis=1, concat_axis=0, tiled=True)
    mirror = moved.transpose(1, 0, 2).reshape(m_dev, ab_dev)
    summed = total + mirror
    squares = lax.psum(jnp.sum(summed * summed, axis=1), "row")
    row_norm = jnp.sqrt(squares / (ab_dev * lax.axis_size("row")) + 1e-06)
    return (summed / row_norm[:, None], row_norm)


def solution(mesh):
    return jax.shard_map(
        local,
        mesh=mesh,
        in_specs=(P("row", "col"), P("col", "row"), P(), P()),
        out_specs=(P("col", "row"), P("col")),
        check_vma=False,
    )
```

profile of v0, /device:TPU:2, one launch (start us, length us, event | category | flops | bytes accessed | tf_op | source)
XLA Modules:
  0.0 403.9 jit_solution(1154354201146444259)
XLA Ops:
  7.2 0.0 all-gather.4.cloned.1.call-start
  7.2 0.7 all-gather.4.cloned.1.call-update
  7.9 0.0 all-gather.6.cloned.1.call-start
  8.0 1.0 convolution_convert_fusion.1
  9.0 0.1 copy.9
  9.1 0.1 broadcast_in_dim.6
  9.2 1.6 bitcast_multiply_fusion.2
  10.8 0.0 all-gather.6.cloned.1.call-update
  10.9 1.3 convolution_convert_fusion
  12.1 0.3 copy.10
  12.4 31.8 %all-gather.4.cloned.1.call-done = bf16[2048,256]{1,0:T(8,128)(2,1)} async-done(((bf16[256,256]{1,0:T(8,128)(2,1)}), bf16[2048,256]{1,0:T(8,128)(2,1)}) %all-gather.4.cloned.1.call-update) | async-done | bytes 1048592 | tf_op jit(solution)/shard_map/all_gather | solution.py:36
  44.2 160.9 %all-gather.6.cloned.1.call-done = bf16[2048,2048]{1,0:T(8,128)(2,1)} async-done(((bf16[32,2048]{1,0:T(8,128)(2,1)}), bf16[2048,2048]{1,0:T(8,128)(2,1)}) %all-gather.6.cloned.1.call-update) | async-done | bytes 8388624 | tf_op jit(solution)/shard_map/all_gather | solution.py:38
  205.1 5.8 %broadcast_in_dim.16 = bf16[2048,2,128]{2,1,0:T(2,128)(2,1)S(1)} broadcast(bf16[2048,2]{1,0:T(8,128)(2,1)S(1)} %copy.10), dimensions={0,1} | broadcast | bytes 1056768 | tf_op jit(solution)/shard_map/broadcast_in_dim | solution.py:21
  210.9 6.1 %fusion = f32[2048,256]{1,0:T(8,128)S(1)} fusion(bf16[2048,2048]{1,0:T(8,128)(2,1)} %all-gather.6.cloned.1.call-done, bf16[2048,256]{1,0:T(8,128)(2,1)} %all-gather.4.cloned.1.call-done, bf16[256,8,2,128]{3,2,1,0:T(2,128)(2,1)S(1)} %bitcast.24), kind=kOutput, calls=%fused_computation.5 | convolution fusion | flops 2148007936 | bytes 12582912 | tf_op jit(solution)/shard_map/dot_general | solution.py:11
  217.0 1.2 copy.11
  218.3 30.6 %all_to_all.18 = f32[16,128,256]{2,0,1:T(8,128)S(1)} all-to-all(f32[16,128,256]{2,0,1:T(8,128)S(1)} %copy.11), channel_id=1, replica_groups=mesh['row'=64,'col'=8] {'col'}, dimensions={1} | all-to-all | bytes 4194304 | tf_op jit(solution)/shard_map/all_to_all | solution.py:40
  248.8 0.2 copy.12
  249.0 0.0 copy-start
  249.0 1.3 copy-done
  250.4 0.4 multiply_reduce_fusion
  250.8 142.9 %psum.7 = f32[2048]{0:T(1024)S(1)} all-reduce(f32[2048]{0:T(1024)S(1)} %multiply_reduce_fusion), channel_id=1, replica_groups=mesh['row'=64,'col'=8] {'row'}, use_global_device_ids=true, to_apply=%region_1.2 | all-reduce | flops 2048 | bytes 16384 | tf_op jit(solution)/shard_map/psum | solution.py:43
  393.8 0.0 copy-start.1
  393.8 3.3 broadcast_divide_fusion
  397.0 0.0 copy-done.1
  (3 shorter events, 0.0 us)
Async XLA Ops:
  7.2 37.0 %all-gather.4.cloned.1.call-start = ((), (), s32[]{:S(2)}) async-start(), calls=%async_computation.1 | async-start | bytes 1179648 | tf_op jit(solution)/shard_map/all_gather | solution.py:36
  7.9 197.2 %all-gather.6.cloned.1.call-start = ((), (), s32[]{:S(2)}) async-start(), calls=%async_computation.2 | async-start | bytes 8519680 | tf_op jit(solution)/shard_map/all_gather | solution.py:38
  249.0 1.3 copy-start
  393.8 3.3 copy-start.1
Sparse Core Ops, SparseCore 0:
  10.1 34.0 all-gather.3
  47.7 157.3 all-gather.5
where the time goes:
time: 404 us
  waiting for transfers between devices  193 us (48%)
  blocking collectives  174 us (43%)
  between operations  14.1 us (3%)
  local copies, waits for them, and re-layouts  9.05 us (2%)
  matrix products  8.42 us (2%)
  other arithmetic  5.29 us (1%)
    all_gather x1, waiting for transfers between devices, local(): lax.all_gather(stacked, 'row', axis=1, tiled=True)[0]  161 us
    psum x1, blocking collectives, local(): squares = lax.psum(jnp.sum(summed * summed, axis=1), 'row')  143 us
    all_gather x1, waiting for transfers between devices, local(): whole_int = lax.all_gather(integrals, 'col', axis=0, tiled=True)  31.8 us
    all_to_all x1, blocking collectives, local(): moved = lax.all_to_all(cube, 'col', split_axis=1, concat_axis=0, tiled=True)  30.6 us
  transfers between devices with their start and end apart: 2, of which 2 were waited for; matrix products, arithmetic and copies ran while one was open for 1% of the time, Pallas kernels for 0%

commit v1 on v0

--- a/solution.py
+++ b/solution.py
@@ -40,7 +40,7 @@
     moved = lax.all_to_all(cube, "col", split_axis=1, concat_axis=0, tiled=True)
     mirror = moved.transpose(1, 0, 2).reshape(m_dev, ab_dev)
     summed = total + mirror
-    squares = lax.psum(jnp.sum(summed * summed, axis=1), "row")
+    squares = jnp.sum(lax.all_gather(jnp.sum(summed * summed, axis=1), "row"), axis=0)
     row_norm = jnp.sqrt(squares / (ab_dev * lax.axis_size("row")) + 1e-06)
     return (summed / row_norm[:, None], row_norm)
 

time: 404 us -> 360 us (0.89)
  blocking collectives: 174 us -> 130 us
    psum x1 -> x0, blocking collectives: 143 us -> none  [local(): squares = lax.psum(jnp.sum(summed * summed, axis=1), 'row')]
    all_gather x0 -> x1, blocking collectives: none -> 99.2 us  [local(): lax.all_gather(jnp.sum(summed * summed, axis=1), 'row')]
where the time goes in v1:
time: 360 us
  waiting for transfers between devices  193 us (54%)
  blocking collectives  130 us (36%)
  between operations  14.1 us (4%)
  local copies, waits for them, and re-layouts  8.72 us (2%)
  matrix products  8.42 us (2%)
  other arithmetic  5.33 us (1%)
    all_gather x1, waiting for transfers between devices, local(): lax.all_gather(stacked, 'row', axis=1, tiled=True)[0]  161 us
    all_gather x1, blocking collectives, local(): lax.all_gather(jnp.sum(summed * summed, axis=1), 'row')  99.2 us
    all_gather x1, waiting for transfers between devices, local(): whole_int = lax.all_gather(integrals, 'col', axis=0, tiled=True)  31.8 us
    all_to_all x1, blocking collectives, local(): moved = lax.all_to_all(cube, 'col', split_axis=1, concat_axis=0, tiled=True)  30.6 us
  transfers between devices with their start and end apart: 2, of which 2 were waited for; matrix products, arithmetic and copies ran while one was open for 1% of the time, Pallas kernels for 0%

profile of v1, /device:TPU:2, one launch (start us, length us, event | category | flops | bytes accessed | tf_op | source)
XLA Modules:
  0.0 359.8 jit_solution(13606656119344552991)
XLA Ops:
  7.2 0.0 all-gather.5.cloned.1.call-start
  7.2 0.7 all-gather.5.cloned.1.call-update
  7.9 0.0 all-gather.7.cloned.1.call-start
  8.0 1.0 convolution_convert_fusion.1
  9.0 0.1 copy.13
  9.1 0.1 broadcast_in_dim.6
  9.2 1.6 bitcast_multiply_fusion.2
  10.8 0.0 all-gather.7.cloned.1.call-update
  10.9 1.3 convolution_convert_fusion
  12.1 0.3 copy.14
  12.4 31.8 %all-gather.5.cloned.1.call-done = bf16[2048,256]{1,0:T(8,128)(2,1)} async-done(((bf16[256,256]{1,0:T(8,128)(2,1)}), bf16[2048,256]{1,0:T(8,128)(2,1)}) %all-gather.5.cloned.1.call-update) | async-done | bytes 1048592 | tf_op jit(solution)/shard_map/all_gather | solution.py:36
  44.2 160.9 %all-gather.7.cloned.1.call-done = bf16[2048,2048]{1,0:T(8,128)(2,1)} async-done(((bf16[32,2048]{1,0:T(8,128)(2,1)}), bf16[2048,2048]{1,0:T(8,128)(2,1)}) %all-gather.7.cloned.1.call-update) | async-done | bytes 8388624 | tf_op jit(solution)/shard_map/all_gather | solution.py:38
  205.1 5.8 %broadcast_in_dim.16 = bf16[2048,2,128]{2,1,0:T(2,128)(2,1)S(1)} broadcast(bf16[2048,2]{1,0:T(8,128)(2,1)S(1)} %copy.14), dimensions={0,1} | broadcast | bytes 1056768 | tf_op jit(solution)/shard_map/broadcast_in_dim | solution.py:21
  210.9 6.1 %fusion = f32[2048,256]{1,0:T(8,128)S(1)} fusion(bf16[2048,2048]{1,0:T(8,128)(2,1)} %all-gather.7.cloned.1.call-done, bf16[2048,256]{1,0:T(8,128)(2,1)} %all-gather.5.cloned.1.call-done, bf16[256,8,2,128]{3,2,1,0:T(2,128)(2,1)S(1)} %bitcast.24), kind=kOutput, calls=%fused_computation.5 | convolution fusion | flops 2148007936 | bytes 12582912 | tf_op jit(solution)/shard_map/dot_general | solution.py:11
  217.0 1.2 copy.15
  218.3 30.6 %all_to_all.18 = f32[16,128,256]{2,0,1:T(8,128)S(1)} all-to-all(f32[16,128,256]{2,0,1:T(8,128)S(1)} %copy.15), channel_id=1, replica_groups=mesh['row'=64,'col'=8] {'col'}, dimensions={1} | all-to-all | bytes 4194304 | tf_op jit(solution)/shard_map/all_to_all | solution.py:40
  248.8 0.2 copy.16
  249.0 0.0 copy-start
  249.0 0.4 multiply_reduce_fusion
  249.5 0.9 copy-done
  250.4 99.2 %all-gather.1 = f32[131072]{0:T(1024)S(1)} all-gather(f32[2048]{0:T(1024)S(1)} %multiply_reduce_fusion), channel_id=3, replica_groups=mesh['row'=64,'col'=8] {'row'}, dimensions={0}, use_global_device_ids=true | all-gather | bytes 532480 | tf_op jit(solution)/shard_map/all_gather | solution.py:43
  349.5 0.1 reshape.54
  349.7 0.0 copy-start.1
  349.7 3.3 broadcast_divide_fusion
  (5 shorter events, 0.1 us)
Async XLA Ops:
  7.2 37.0 %all-gather.5.cloned.1.call-start = ((), (), s32[]{:S(2)}) async-start(), calls=%async_computation.1 | async-start | bytes 1179648 | tf_op jit(solution)/shard_map/all_gather | solution.py:36
  7.9 197.2 %all-gather.7.cloned.1.call-start = ((), (), s32[]{:S(2)}) async-start(), calls=%async_computation.2 | async-start | bytes 8519680 | tf_op jit(solution)/shard_map/all_gather | solution.py:38
  249.0 1.3 copy-start
  349.7 3.3 copy-start.1
Sparse Core Ops, SparseCore 0:
  10.1 34.0 all-gather.4
  47.7 157.3 all-gather.6
